TPU v7x, 32 devices: a whole 2x2x4 slice. The times are simulated.
32 devices in a mesh: dp: 16 (over z, y, core), tensor: 2 (over x).
Axes of the slice: x: 2, y: 2, z: 4, core: 2. Of those that a mesh axis runs over, the one named last changes fastest.
Arguments:
- frames_in: bfloat16 [2, 16, 1024, 1024], P(None, 'dp', 'tensor'), may hold values from -6 to 6
- phone_len: int32 [2, 16], P(None, 'dp'), may hold values from 10 to 204
- frame_len: int32 [2, 16], P(None, 'dp'), may hold values from 512 to 819
- section: int32 [2, 16], P(None, 'dp'), may hold values from 0 to 6
- norm_gain: float32 [2, 1024], replicated, may hold values from 0.5 to 1.5
- norm_bias: float32 [2, 1024], replicated, may hold values from -4 to 4
- ada_scale: float32 [2, 7, 1024], replicated, may hold values from 0.5 to 1.5
- ada_shift: float32 [2, 7, 1024], replicated, may hold values from -4 to 4
- w_qkv: bfloat16 [2, 1024, 3, 1024], P(None, None, None, 'tensor'), may hold values from -0.1875 to 0.1875
- w_out: bfloat16 [2, 1024, 1024], P(None, 'tensor'), may hold values from -4 to 4
- w_up: bfloat16 [2, 1024, 4096], P(None, None, 'tensor'), may hold values from -0.1875 to 0.1875
- w_down: bfloat16 [2, 4096, 1024], P(None, 'tensor'), may hold values from -0.09375 to 0.09375
- out_grad: bfloat16 [2, 16, 1024, 1024], P(None, 'dp', 'tensor'), may hold values from -6 to 6
Outputs:
- frames_out: float32 [2, 16, 1024, 1024], P(None, 'dp', 'tensor')
- frames_grad: float32 [2, 16, 1024, 1024], P(None, 'dp', 'tensor')
- grad_qkv: float32 [2, 1024, 3, 1024], P(None, None, None, 'tensor')
- grad_out: float32 [2, 1024, 1024], P(None, 'tensor')
- grad_up: float32 [2, 1024, 4096], P(None, None, 'tensor')
- grad_down: float32 [2, 4096, 1024], P(None, 'tensor')
- grad_norm_gain: float32 [2, 1024], replicated
- grad_norm_bias: float32 [2, 1024], replicated
- grad_ada_scale: float32 [2, 7, 1024], replicated
- grad_ada_shift: float32 [2, 7, 1024], replicated
All inputs are finite; a program needn't handle non-finite values.
Results may differ from a plain program's by a relative error of at most 0.028.
Values may be sent and summed in bfloat16 or wider, within the bound.
No kernel may reach another device: no remote copies, remote signals or barrier semaphores. Data moves between devices by JAX's collectives and lax.ppermute only.
A program may use at most 384 MiB of HBM per device.

v0:
```python
from functools import partial
import jax
import jax.numpy as jnp
from jax import lax
from jax.sharding import PartitionSpec as P

HEAD_DIM = 64
norm_eps = 1e-05
masked_score = -1000000000.0
contract_rows = (((0,), (0,)), ((), ()))
contract_cols = (((1,), (1,)), ((), ()))


def plain_norm(inputs):
    centered = inputs - jnp.mean(inputs, axis=-1, keepdims=True)
    variance = jnp.mean(centered * centered, axis=-1, keepdims=True)
    return centered * lax.rsqrt(variance + norm_eps)


def fixed_norm(inputs, gain_row, shift_row):
    return plain_norm(inputs) * gain_row + shift_row


def section_norm(inputs, scale_table, shift_table, picker):
    scale_row = jnp.dot(
        picker, scale_table, precision=lax.Precision.HIGHEST, preferred_element_type=jnp.float32
    )
    shift_row = jnp.dot(
        picker, shift_table, precision=lax.Precision.HIGHEST, preferred_element_type=jnp.float32
    )
    return plain_norm(inputs) * scale_row + shift_row


def gather_normed(normed_low):
    return lax.all_gather(normed_low, "tensor", axis=0, tiled=True)


def gather_again(normed_low):
    return lax.all_gather(normed_low, "tensor", axis=0, tiled=True)


def sum_branch(branch_part):
    return lax.psum_scatter(
        branch_part.astype(jnp.bfloat16), "tensor", scatter_dimension=0, tiled=True
    ).astype(jnp.float32)


def gather_grad(grad_low):
    return lax.all_gather(grad_low, "tensor", axis=0, tiled=True)


def sum_normed(grad_part):
    return lax.psum_scatter(
        grad_part.astype(jnp.bfloat16), "tensor", scatter_dimension=0, tiled=True
    ).astype(jnp.float32)


def key_allowed(query_pos, key_pos, prefix, valid_count, causal):
    allowed = key_pos[None, :] < valid_count
    if causal:
        allowed = allowed & ((key_pos[None, :] < prefix) | (key_pos[None, :] <= query_pos[:, None]))
    return allowed


def split_heads(projected):
    length = projected.shape[0]
    head_width = projected.shape[1] // 3
    head_count = head_width // HEAD_DIM
    query_rows = projected[:, :head_width].reshape(length, head_count, HEAD_DIM)
    key_rows = projected[:, head_width : 2 * head_width].reshape(length, head_count, HEAD_DIM)
    value_rows = projected[:, 2 * head_width :].reshape(length, head_count, HEAD_DIM)
    return (query_rows, key_rows, value_rows)


def block_scores(query_block, key_rows, block_start, prefix, valid_count, causal):
    block_rows = query_block.shape[0]
    length = key_rows.shape[0]
    scores = jnp.einsum(
        "qhd,khd->hqk", query_block, key_rows, preferred_element_type=jnp.float32
    ) * HEAD_DIM ** (-0.5)
    query_pos = block_start + lax.iota(jnp.int32, block_rows)
    key_pos = lax.iota(jnp.int32, length)
    allowed = key_allowed(query_pos, key_pos, prefix, valid_count, causal)
    return jnp.where(allowed[None], scores, masked_score)


def attend_forward(projected, prefix, valid_count, causal, block_rows):
    length = projected.shape[0]
    head_width = projected.shape[1] // 3
    query_rows, key_rows, value_rows = split_heads(projected)

    def one_block(block_start):
        query_block = lax.dynamic_slice_in_dim(query_rows, block_start, block_rows, 0)
        scores = block_scores(query_block, key_rows, block_start, prefix, valid_count, causal)
        highest = jnp.max(scores, axis=-1, keepdims=True)
        row_total = jnp.sum(jnp.exp(scores - highest), axis=-1, keepdims=True)
        log_total = highest + jnp.log(row_total)
        shares = jnp.exp(scores - log_total).astype(jnp.bfloat16)
        mixture = jnp.einsum("hqk,khd->qhd", shares, value_rows, preferred_element_type=jnp.float32)
        return (mixture.astype(jnp.bfloat16), log_total)

    starts = lax.iota(jnp.int32, length // block_rows) * block_rows
    mixture, log_totals = lax.map(one_block, starts)
    return (mixture.reshape(length, head_width), log_totals)


def attend_backward(projected, log_totals, grad_mixture, prefix, valid_count, causal, block_rows):
    length = projected.shape[0]
    head_width = projected.shape[1] // 3
    query_rows, key_rows, value_rows = split_heads(projected)
    grad_rows = grad_mixture.reshape(query_rows.shape)
    score_scale = HEAD_DIM ** (-0.5)

    def one_block(grad_state, block_item):
        block_start, log_total = block_item
        grad_key, grad_value = grad_state
        query_block = lax.dynamic_slice_in_dim(query_rows, block_start, block_rows, 0)
        grad_block = lax.dynamic_slice_in_dim(grad_rows, block_start, block_rows, 0)
        scores = block_scores(query_block, key_rows, block_start, prefix, valid_count, causal)
        shares = jnp.exp(scores - log_total)
        shares_low = shares.astype(jnp.bfloat16)
        grad_shares = jnp.einsum(
            "qhd,khd->hqk", grad_block, value_rows, preferred_element_type=jnp.float32
        )
        inner_sum = jnp.sum(shares * grad_shares, axis=-1, keepdims=True)
        grad_scores = (shares * (grad_shares - inner_sum)).astype(jnp.bfloat16)
        grad_query = (
            jnp.einsum("hqk,khd->qhd", grad_scores, key_rows, preferred_element_type=jnp.float32)
            * score_scale
        )
        grad_key = (
            grad_key
            + jnp.einsum(
                "hqk,qhd->khd", grad_scores, query_block, preferred_element_type=jnp.float32
            )
            * score_scale
        )
        grad_value = grad_value + jnp.einsum(
            "hqk,qhd->khd", shares_low, grad_block, preferred_element_type=jnp.float32
        )
        return ((grad_key, grad_value), grad_query)

    starts = lax.iota(jnp.int32, length // block_rows) * block_rows
    zero_rows = jnp.zeros(query_rows.shape, jnp.float32)
    grad_state, grad_query = lax.scan(one_block, (zero_rows, zero_rows), (starts, log_totals))
    grad_key, grad_value = grad_state
    joined = jnp.concatenate(
        [
            grad_query.reshape(length, head_width),
            grad_key.reshape(length, head_width),
            grad_value.reshape(length, head_width),
        ],
        axis=1,
    )
    return joined.astype(jnp.bfloat16)


def per_device(
    frames_in,
    phone_len,
    frame_len,
    section,
    norm_gain,
    norm_bias,
    ada_scale,
    ada_shift,
    w_qkv,
    w_out,
    w_up,
    w_down,
    out_grad,
):
    micro_count, local_seqs, local_rows, model_width = frames_in.shape
    seq_length = local_rows * lax.axis_size("tensor")
    block_rows = min(512, seq_length)
    section_count = ada_scale.shape[1]
    qkv_mats = [w_qkv[layer_index].reshape(model_width, -1) for layer_index in range(2)]
    acc_qkv = [jnp.zeros(qkv_mats[layer_index].shape, jnp.float32) for layer_index in range(2)]
    acc_out = [jnp.zeros(w_out.shape[1:], jnp.float32) for layer_index in range(2)]
    acc_up = [jnp.zeros(w_up.shape[1:], jnp.float32) for layer_index in range(2)]
    acc_down = [jnp.zeros(w_down.shape[1:], jnp.float32) for layer_index in range(2)]
    acc_gain = [jnp.zeros((model_width,), jnp.float32) for part_index in range(2)]
    acc_bias = [jnp.zeros((model_width,), jnp.float32) for part_index in range(2)]
    acc_scale = [jnp.zeros((section_count, model_width), jnp.float32) for part_index in range(2)]
    acc_shift = [jnp.zeros((section_count, model_width), jnp.float32) for part_index in range(2)]
    frames_list = []
    grads_list = []
    for micro_index in range(micro_count):
        prefix = phone_len[micro_index, 0]
        valid_count = prefix + frame_len[micro_index, 0]
        picker = (lax.iota(jnp.int32, section_count) == section[micro_index, 0]).astype(
            jnp.float32
        )[None, :]
        residual = frames_in[micro_index, 0].astype(jnp.float32)
        stored = []
        for layer_index in range(2):
            for part_index in range(2):
                if layer_index == 0:
                    normed, norm_back = jax.vjp(
                        fixed_norm, residual, norm_gain[part_index], norm_bias[part_index]
                    )
                else:
                    normed, norm_back = jax.vjp(
                        partial(section_norm, picker=picker),
                        residual,
                        ada_scale[part_index],
                        ada_shift[part_index],
                    )
                normed_low = normed.astype(jnp.bfloat16)
                gathered = gather_normed(normed_low)
                if part_index == 0:
                    projected = jnp.dot(
                        gathered, qkv_mats[layer_index], preferred_element_type=jnp.float32
                    ).astype(jnp.bfloat16)
                    mixture, log_totals = attend_forward(
                        projected, prefix, valid_count, layer_index == 0, block_rows
                    )
                    branch = sum_branch(
                        jnp.dot(mixture, w_out[layer_index], preferred_element_type=jnp.float32)
                    )
                    saved_state = (projected, log_totals, mixture)
                else:
                    hidden = jnp.dot(
                        gathered, w_up[layer_index], preferred_element_type=jnp.float32
                    )
                    active = jax.nn.gelu(hidden, approximate=True).astype(jnp.bfloat16)
                    branch = sum_branch(
                        jnp.dot(active, w_down[layer_index], preferred_element_type=jnp.float32)
                    )
                    saved_state = (hidden, active)
                kept_rows = normed_low
                stored.append((norm_back, kept_rows, saved_state))
                residual = residual + branch
        out_group = [residual]
        grad_rows = out_grad[micro_index, 0].astype(jnp.float32)
        for layer_index in (1, 0):
            for part_index in (1, 0):
                norm_back, kept_rows, saved_state = stored[2 * layer_index + part_index]
                gathered = gather_again(kept_rows)
                grad_whole = gather_grad(grad_rows.astype(jnp.bfloat16))
                if part_index == 1:
                    hidden, active = saved_state
                    acc_down[layer_index] = acc_down[layer_index] + lax.dot_general(
                        active, grad_whole, contract_rows, preferred_element_type=jnp.float32
                    )
                    grad_active = lax.dot_general(
                        grad_whole,
                        w_down[layer_index],
                        contract_cols,
                        preferred_element_type=jnp.float32,
                    )
                    gelu_value, gelu_back = jax.vjp(partial(jax.nn.gelu, approximate=True), hidden)
                    grad_hidden = gelu_back(grad_active)[0].astype(jnp.bfloat16)
                    acc_up[layer_index] = acc_up[layer_index] + lax.dot_general(
                        gathered, grad_hidden, contract_rows, preferred_element_type=jnp.float32
                    )
                    grad_normed = sum_normed(
                        lax.dot_general(
                            grad_hidden,
                            w_up[layer_index],
                            contract_cols,
                            preferred_element_type=jnp.float32,
                        )
                    )
                else:
                    projected, log_totals, mixture = saved_state
                    acc_out[layer_index] = acc_out[layer_index] + lax.dot_general(
                        mixture, grad_whole, contract_rows, preferred_element_type=jnp.float32
                    )
                    grad_mixture = lax.dot_general(
                        grad_whole,
                        w_out[layer_index],
                        contract_cols,
                        preferred_element_type=jnp.float32,
                    ).astype(jnp.bfloat16)
                    grad_projected = attend_backward(
                        projected,
                        log_totals,
                        grad_mixture,
                        prefix,
                        valid_count,
                        layer_index == 0,
                        block_rows,
                    )
                    acc_qkv[layer_index] = acc_qkv[layer_index] + lax.dot_general(
                        gathered, grad_projected, contract_rows, preferred_element_type=jnp.float32
                    )
                    grad_normed = sum_normed(
                        lax.dot_general(
                            grad_projected,
                            qkv_mats[layer_index],
                            contract_cols,
                            preferred_element_type=jnp.float32,
                        )
                    )
                grad_input, grad_first, grad_second = norm_back(grad_normed)
                grad_rows = grad_rows + grad_input
                if layer_index == 0:
                    acc_gain[part_index] = acc_gain[part_index] + grad_first
                    acc_bias[part_index] = acc_bias[part_index] + grad_second
                else:
                    acc_scale[part_index] = acc_scale[part_index] + grad_first
                    acc_shift[part_index] = acc_shift[part_index] + grad_second
        grad_group = [grad_rows]
        frames_list.append(jnp.stack(out_group))
        grads_list.append(jnp.stack(grad_group))
    total_qkv, total_out, total_up, total_down = (
        lax.psum(jnp.stack(acc_qkv).astype(jnp.bfloat16), "dp").astype(jnp.float32),
        lax.psum(jnp.stack(acc_out).astype(jnp.bfloat16), "dp").astype(jnp.float32),
        lax.psum(jnp.stack(acc_up).astype(jnp.bfloat16), "dp").astype(jnp.float32),
        lax.psum(jnp.stack(acc_down).astype(jnp.bfloat16), "dp").astype(jnp.float32),
    )
    norm_totals = lax.psum(
        (jnp.stack(acc_gain), jnp.stack(acc_bias), jnp.stack(acc_scale), jnp.stack(acc_shift)),
        ("dp", "tensor"),
    )
    return (
        jnp.stack(frames_list),
        jnp.stack(grads_list),
        total_qkv.reshape(2, model_width, 3, -1),
        total_out,
        total_up,
        total_down,
        norm_totals[0],
        norm_totals[1],
        norm_totals[2],
        norm_totals[3],
    )


def solution(mesh):
    return jax.shard_map(
        per_device,
        mesh=mesh,
        in_specs=(
            P(None, "dp", "tensor", None),
            P(None, "dp"),
            P(None, "dp"),
            P(None, "dp"),
            P(),
            P(),
            P(),
            P(),
            P(None, None, None, "tensor"),
            P(None, "tensor", None),
            P(None, None, "tensor"),
            P(None, "tensor", None),
            P(None, "dp", "tensor", None),
        ),
        out_specs=(
            P(None, "dp", "tensor", None),
            P(None, "dp", "tensor", None),
            P(None, None, None, "tensor"),
            P(None, "tensor", None),
            P(None, None, "tensor"),
            P(None, "tensor", None),
            P(),
            P(),
            P(),
            P(),
        ),
        check_vma=False,
    )
```

profile of v0, /device:TPU:0, one launch (start us, length us, event | category | flops | bytes accessed | tf_op | source)
XLA Modules:
  0.0 2267.6 jit_solution(17285633225396595511)
XLA Ops:
  28.0 22.1 all-gather.19.cloned.1.call-done
  63.6 38.0 %while.108 = (s32[]{:T(128)}, bf16[2,512,8,64]{1,3,2,0:T(8,128)(2,1)S(1)}, f32[2,8,512,1]{2,1,3,0:T(8,128)S(1)}, s32[]{:T(128)}, s32[]{:T(128)}, /*index=5*/s32[...) while((s32[]{:T(128)}, ...), condition=%wide.region_5.6_spmd, body=%wide.region_2.5_spmd.sunk | while | flops 1121712640 | bytes 55713984 | solution.py:103
  106.9 31.7 %reduce-scatter.17.cloned.1.call-done = bf16[512,1024]{1,0:T(8,128)(2,1)} async-done(((bf16[1024,1024]{1,0:T(8,128)(2,1)}), bf16[512,1024]{1,0:T(8,128)(2,1)}) %reduce-scatter.17.cloned.1.call-update) | async-done | bytes 1048592 | tf_op jit(solution)/shard_map/reduce_scatter | solution.py:43
  143.3 31.9 %all-gather.27.cloned.1.call-done = bf16[1024,1024]{1,0:T(8,128)(2,1)} async-done(((bf16[512,1024]{1,0:T(8,128)(2,1)}), bf16[1024,1024]{1,0:T(8,128)(2,1)}) %all-gather.27.cloned.1.call-update) | async-done | bytes 2097168 | tf_op jit(solution)/shard_map/all_gather | solution.py:35
  188.8 38.0 %while.110 = (s32[]{:T(128)}, bf16[2,512,8,64]{1,3,2,0:T(8,128)(2,1)S(1)}, f32[2,8,512,1]{2,1,3,0:T(8,128)S(1)}, s32[]{:T(128)}, s32[]{:T(128)}, /*index=5*/s32[...) while((s32[]{:T(128)}, ...), condition=%wide.region_25.26_spmd, body=%wide.region_22.25_spmd.sunk | while | flops 1121712640 | bytes 55713984 | solution.py:103
  232.1 31.7 %reduce-scatter.25.cloned.1.call-done = bf16[512,1024]{1,0:T(8,128)(2,1)} async-done(((bf16[1024,1024]{1,0:T(8,128)(2,1)}), bf16[512,1024]{1,0:T(8,128)(2,1)}) %reduce-scatter.25.cloned.1.call-update) | async-done | bytes 1048592 | tf_op jit(solution)/shard_map/reduce_scatter | solution.py:43
  269.9 32.6 %all-gather.29.cloned.1.call-done = bf16[1024,1024]{1,0:T(8,128)(2,1)} async-done(((bf16[512,1024]{1,0:T(8,128)(2,1)}), bf16[1024,1024]{1,0:T(8,128)(2,1)}) %all-gather.29.cloned.1.call-update) | async-done | bytes 2097168 | tf_op jit(solution)/shard_map/all_gather | solution.py:35
  322.4 15.3 all-gather.21.cloned.1.call-done
  360.2 12.1 reduce-scatter.27.cloned.1.call-done
  372.3 34.8 %reduce-scatter.19.cloned.1.call-done = bf16[512,1024]{1,0:T(8,128)(2,1)} async-done(((bf16[1024,1024]{1,0:T(8,128)(2,1)}), bf16[512,1024]{1,0:T(8,128)(2,1)}) %reduce-scatter.19.cloned.1.call-update) | async-done | bytes 1048592 | tf_op jit(solution)/shard_map/reduce_scatter | solution.py:43
  422.0 25.1 %all-gather.31.cloned.1.call-done = bf16[1024,1024]{1,0:T(8,128)(2,1)} async-done(((bf16[512,1024]{1,0:T(8,128)(2,1)}), bf16[1024,1024]{1,0:T(8,128)(2,1)}) %all-gather.31.cloned.1.call-update) | async-done | bytes 2097168 | tf_op jit(solution)/shard_map/all_gather | solution.py:35
  457.0 25.2 %all-gather.23.cloned.1.call-done = bf16[1024,1024]{1,0:T(8,128)(2,1)} async-done(((bf16[512,1024]{1,0:T(8,128)(2,1)}), bf16[1024,1024]{1,0:T(8,128)(2,1)}) %all-gather.23.cloned.1.call-update) | async-done | bytes 2097168 | tf_op jit(solution)/shard_map/all_gather | solution.py:35
  495.9 31.0 %while.109 = (s32[]{:T(128)}, bf16[2,512,8,64]{1,3,2,0:T(8,128)(2,1)}, f32[2,8,512,1]{2,1,3,0:T(8,128)S(1)}, s32[]{:T(128)}, s32[2]{0:T(128)S(1)}, /*index=5*/bf...) while((s32[]{:T(128)}, ...), condition=%wide.region_15.16_spmd, body=%wide.region_12.15_spmd.sunk | while | flops 1120138240 | bytes 66195716 | solution.py:103
  535.1 28.7 %while.111 = (s32[]{:T(128)}, bf16[2,512,8,64]{1,3,2,0:T(8,128)(2,1)}, f32[2,8,512,1]{2,1,3,0:T(8,128)S(1)}, s32[]{:T(128)}, s32[2]{0:T(128)S(1)}, /*index=5*/bf...) while((s32[]{:T(128)}, ...), condition=%wide.region_35.36_spmd, body=%wide.region_32.35_spmd.sunk | while | flops 1120138240 | bytes 62001388 | solution.py:103
  582.2 20.7 reduce-scatter.29.cloned.1.call-done
  607.2 30.9 %all-gather.25.cloned.1.call-done = bf16[1024,1024]{1,0:T(8,128)(2,1)} async-done(((bf16[512,1024]{1,0:T(8,128)(2,1)}), bf16[1024,1024]{1,0:T(8,128)(2,1)}) %all-gather.25.cloned.1.call-update) | async-done | bytes 2097168 | tf_op jit(solution)/shard_map/all_gather | solution.py:35
  638.2 10.9 fusion.158
  649.1 24.2 %all-gather.47.cloned.1.call-done = bf16[1,1,1024,1024]{3,2,1,0:T(8,128)(2,1)} async-done(((bf16[1,1,512,1024]{3,2,1,0:T(8,128)(2,1)}), bf16[1,1,1024,1024]{3,2,1,0:T(8,128)(2,1)}) %all-gather.47.cloned.1.call-update) | async-done | bytes 2097168 | tf_op jit(solution)/shard_map/all_gather | solution.py:49
  673.3 12.5 fusion.125
  696.2 11.0 fusion.275
  708.4 10.8 fusion.156
  719.2 23.7 %reduce-scatter.33.cloned.1.call-done = bf16[512,1024]{1,0:T(8,128)(2,1)} async-done(((bf16[1024,1024]{1,0:T(8,128)(2,1)}), bf16[512,1024]{1,0:T(8,128)(2,1)}) %reduce-scatter.33.cloned.1.call-update) | async-done | bytes 1048592 | tf_op jit(solution)/shard_map/reduce_scatter | solution.py:53
  745.6 31.3 %reduce-scatter.23.cloned.1.call-done = bf16[512,1024]{1,0:T(8,128)(2,1)} async-done(((bf16[1024,1024]{1,0:T(8,128)(2,1)}), bf16[512,1024]{1,0:T(8,128)(2,1)}) %reduce-scatter.23.cloned.1.call-update) | async-done | bytes 1048592 | tf_op jit(solution)/shard_map/reduce_scatter | solution.py:43
  783.4 28.2 %all-gather.49.cloned.1.call-done = bf16[1,1,1024,1024]{3,2,1,0:T(8,128)(2,1)} async-done(((bf16[1,1,512,1024]{3,2,1,0:T(8,128)(2,1)}), bf16[1,1,1024,1024]{3,2,1,0:T(8,128)(2,1)}) %all-gather.49.cloned.1.call-update) | async-done | bytes 2097168 | tf_op jit(solution)/shard_map/all_gather | solution.py:49
  811.5 12.5 fusion.139
  834.3 11.1 fusion.278
  851.8 86.9 %while.112 = (s32[]{:T(128)}, f32[1024,8,64]{0,2,1:T(8,128)}, f32[1024,8,64]{0,2,1:T(8,128)}, bf16[2,512,8,64]{1,3,2,0:T(8,128)(2,1)}, s32[2]{0:T(128)S(1)}, /*i...) while((s32[]{:T(128)}, f32[1024,8,64]{0,2,1:T(8,128)}, ...), condition=%wide.region_45.46_spmd.clone, body=%wide.region_43.45_spmd.clone.sunk | while | flops 2724983808 | bytes 207702432 | solution.py:145
  860.0 10.8 multiply_reduce_fusion.14
  870.8 9.5 multiply_convert_fusion.20
  902.9 10.8 multiply_reduce_fusion.14
  913.7 9.5 multiply_convert_fusion.20
  923.2 9.5 bitcast_add_fusion.17
  959.3 23.0 %reduce-scatter.35.cloned.1.call-done = bf16[512,1024]{1,0:T(8,128)(2,1)} async-done(((bf16[1024,1024]{1,0:T(8,128)(2,1)}), bf16[512,1024]{1,0:T(8,128)(2,1)}) %reduce-scatter.35.cloned.1.call-update) | async-done | bytes 1048592 | tf_op jit(solution)/shard_map/reduce_scatter | solution.py:53
  991.6 33.2 %all-gather.41.cloned.1.call-done = bf16[1024,1024]{1,0:T(8,128)(2,1)} async-done(((bf16[512,1024]{1,0:T(8,128)(2,1)}), bf16[1024,1024]{1,0:T(8,128)(2,1)}) %all-gather.41.cloned.1.call-update) | async-done | bytes 2097168 | tf_op jit(solution)/shard_map/all_gather | solution.py:49
  1030.1 86.5 %while.114 = (s32[]{:T(128)}, f32[1024,8,64]{0,2,1:T(8,128)}, f32[1024,8,64]{0,2,1:T(8,128)}, bf16[2,512,8,64]{1,3,2,0:T(8,128)(2,1)}, s32[2]{0:T(128)S(1)}, /*i...) while((s32[]{:T(128)}, f32[1024,8,64]{0,2,1:T(8,128)}, ...), condition=%wide.region_63.64_spmd.clone, body=%wide.region_61.63_spmd.clone.sunk | while | flops 2724983808 | bytes 207702432 | solution.py:145
  1038.1 10.8 multiply_reduce_fusion.16
  1080.9 10.8 multiply_reduce_fusion.16
  1137.2 11.8 fusion.143
  1149.1 10.9 fusion.382
  1167.0 27.6 %all-gather.37.cloned.1.call-done = bf16[1024,1024]{1,0:T(8,128)(2,1)} async-done(((bf16[512,1024]{1,0:T(8,128)(2,1)}), bf16[1024,1024]{1,0:T(8,128)(2,1)}) %all-gather.37.cloned.1.call-update) | async-done | bytes 2097168 | tf_op jit(solution)/shard_map/all_gather | solution.py:49
  1194.6 12.5 fusion.118
  1217.4 12.0 fusion.141
  1236.6 13.2 fusion.132
  1280.7 12.9 fusion.355
  1308.6 14.1 fusion.142
  1346.4 114.4 %while.115 = (s32[]{:T(128)}, f32[1024,8,64]{0,2,1:T(8,128)}, f32[1024,8,64]{0,2,1:T(8,128)}, bf16[2,512,8,64]{1,3,2,0:T(8,128)(2,1)}, s32[2]{0:T(128)S(1)}, /*i...) while((s32[]{:T(128)}, f32[1024,8,64]{0,2,1:T(8,128)}, ...), condition=%wide.region_72.73_spmd.clone, body=%wide.region_70.72_spmd.clone.sunk | while | flops 2726558208 | bytes 225534288 | solution.py:145
  1350.9 10.2 fusion.588
  1361.2 13.5 multiply_reduce_fusion.17
  1374.7 11.5 multiply_convert_fusion.23
  1407.6 10.0 fusion.588
  1417.6 13.5 multiply_reduce_fusion.17
  1431.1 11.5 multiply_convert_fusion.23
  1476.4 114.0 %while.113 = (s32[]{:T(128)}, f32[1024,8,64]{0,2,1:T(8,128)}, f32[1024,8,64]{0,2,1:T(8,128)}, bf16[2,512,8,64]{1,3,2,0:T(8,128)(2,1)}, s32[2]{0:T(128)S(1)}, /*i...) while((s32[]{:T(128)}, f32[1024,8,64]{0,2,1:T(8,128)}, ...), condition=%wide.region_54.55_spmd.clone, body=%wide.region_52.54_spmd.clone.sunk | while | flops 2726558208 | bytes 225534288 | solution.py:145
  1480.8 10.1 fusion.565
  1490.9 13.6 multiply_reduce_fusion.15
  1504.5 11.5 multiply_convert_fusion.21
  1537.5 10.0 fusion.565
  1547.5 13.5 multiply_reduce_fusion.15
  1561.0 11.5 multiply_convert_fusion.21
  1600.6 12.0 fusion.140
  1673.6 98.0 %all-reduce.5.cloned.1.call-done = (f32[2,1024]{1,0:T(2,128)}, f32[2,1024]{1,0:T(2,128)}, f32[2,7,1024]{2,1,0:T(8,128)}, f32[2,7,1024]{2,1,0:T(8,128)}) async-done(((f32[2,1024]{1,0:T(2,128)}, f32[2,1024]{1,0:T(2,128)}, f32[2,7,1024]{2,1,0:T(8,128)}, f32[2,7,1024]{2,1,0:T(8,128)}), (f32[2,1024]{1,0:T(2,128)}, f32[2,1024]{1,0:T(2,128)}, f32[2,7,1024]{2,1,0:T(8,128)}, ...) | async-done | bytes 131088 | tf_op jit(solution)/shard_map/psum | solution.py:313
  1774.6 447.7 %all-reduce.7.cloned.1.call-done = (bf16[2,1024,3,512]{1,3,2,0:T(8,128)(2,1)}, bf16[2,512,1024]{2,1,0:T(8,128)(2,1)}, bf16[2,1024,2048]{2,1,0:T(8,128)(2,1)}, bf16[2,2048,1024]{2,1,0:T(8,128)(2,1)}) async-done(((bf16[2,1024,3,512]{1,3,2,0:T(8,128)(2,1)}, bf16[2,512,1024]{2,1,0:T(8,128)(2,1)}, bf16[2,1024,2048]{2,1,0:T(8,128)(2,1)}, bf16[2,2048,1024]{2,1,0:T(8,128)(2,1)}), ...) | async-done | bytes 25165840 | tf_op jit(solution)/shard_map/psum | solution.py:308
  2235.7 11.7 convert_element_type.355
  2247.4 11.7 convert_element_type.356
  (902 shorter events, 759.0 us)
Async XLA Ops:
  7.2 42.9 %all-gather.19.cloned.1.call-start = ((), (), s32[]{:S(2)}) async-start(), calls=%async_computation.16 | async-start | bytes 3145728 | tf_op jit(solution)/shard_map/all_gather | solution.py:35
  12.1 128.4 %copy-start.116 = (f32[1,1024]{1,0:T(1,128)}, f32[1,1024]{1,0:T(1,128)S(1)}, u32[]{:S(2)}) copy-start(f32[1,1024]{1,0:T(1,128)S(1)} %get-tuple-element.998) | copy-start | bytes 12292
  14.1 124.5 %reduce-scatter.17.cloned.1.call-start = ((), (), s32[]{:S(2)}) async-start(), calls=%async_computation.17 | async-start | bytes 3145728 | tf_op jit(solution)/shard_map/reduce_scatter | solution.py:43
  106.7 68.6 %all-gather.27.cloned.1.call-start = ((), (), s32[]{:S(2)}) async-start(), calls=%async_computation.24 | async-start | bytes 3145728 | tf_op jit(solution)/shard_map/all_gather | solution.py:35
  106.9 35.1 %copy-start.124 = (f32[512]{0:T(512)}, f32[512]{0:T(512)S(1)}, u32[]{:S(2)}) copy-start(f32[512]{0:T(512)S(1)} %broadcast_multiply_fusion.3) | copy-start | bytes 6148
  140.5 34.8 %copy-start.164 = (f32[512]{0:T(512)}, f32[512]{0:T(512)S(1)}, u32[]{:S(2)}) copy-start(f32[512]{0:T(512)S(1)} %get-tuple-element.733) | copy-start | bytes 6148
  140.5 34.7 %copy-start.144 = (f32[512]{0:T(512)}, f32[512]{0:T(512)S(1)}, u32[]{:S(2)}) copy-start(f32[512]{0:T(512)S(1)} %fusion.331) | copy-start | bytes 6148
  142.0 121.8 %reduce-scatter.25.cloned.1.call-start = ((), (), s32[]{:S(2)}) async-start(), calls=%async_computation.25 | async-start | bytes 3145728 | tf_op jit(solution)/shard_map/reduce_scatter | solution.py:43
  229.2 34.6 %copy-start.40 = (bf16[512,1024]{1,0:T(8,128)(2,1)S(1)}, bf16[512,1024]{1,0:T(8,128)(2,1)}, u32[]{:S(2)}) copy-start(bf16[512,1024]{1,0:T(8,128)(2,1)} %reduce-scatter.17.cloned.1.call-done) | copy-start | bytes 3145732
  231.8 70.7 %all-gather.29.cloned.1.call-start = ((), (), s32[]{:S(2)}) async-start(), calls=%async_computation.26 | async-start | bytes 3145728 | tf_op jit(solution)/shard_map/all_gather | solution.py:35
  232.1 34.9 %copy-start.136 = (f32[512]{0:T(512)}, f32[512]{0:T(512)S(1)}, u32[]{:S(2)}) copy-start(f32[512]{0:T(512)S(1)} %broadcast_multiply_fusion.6) | copy-start | bytes 6148
  232.1 34.9 %copy-start.132 = (f32[1,1024]{1,0:T(1,128)S(1)}, f32[1,1024]{1,0:T(1,128)}, u32[]{:S(2)}) copy-start(f32[1,1024]{1,0:T(1,128)} %get-tuple-element.997) | copy-start | bytes 12292
  232.1 34.9 %copy-start.188 = (f32[1,1024]{1,0:T(1,128)S(1)}, f32[1,1024]{1,0:T(1,128)}, u32[]{:S(2)}) copy-start(f32[1,1024]{1,0:T(1,128)} %get-tuple-element.999) | copy-start | bytes 12292
  269.3 68.4 %all-gather.21.cloned.1.call-start = ((), (), s32[]{:S(2)}) async-start(), calls=%async_computation.18 | async-start | bytes 3145728 | tf_op jit(solution)/shard_map/all_gather | solution.py:35
  269.8 102.5 %reduce-scatter.27.cloned.1.call-start = ((), (), s32[]{:S(2)}) async-start(), calls=%async_computation.27 | async-start | bytes 3145728 | tf_op jit(solution)/shard_map/reduce_scatter | solution.py:43
  322.0 85.2 %reduce-scatter.19.cloned.1.call-start = ((), (), s32[]{:S(2)}) async-start(), calls=%async_computation.19 | async-start | bytes 3145728 | tf_op jit(solution)/shard_map/reduce_scatter | solution.py:43
  356.8 90.3 %all-gather.31.cloned.1.call-start = ((), (), s32[]{:S(2)}) async-start(), calls=%async_computation.28 | async-start | bytes 3145728 | tf_op jit(solution)/shard_map/all_gather | solution.py:35
  358.8 52.7 %copy-start.118 = (f32[1,1024]{1,0:T(1,128)}, f32[1,1024]{1,0:T(1,128)S(1)}, u32[]{:S(2)}) copy-start(f32[1,1024]{1,0:T(1,128)S(1)} %fusion.317) | copy-start | bytes 12292
  413.8 68.4 %all-gather.23.cloned.1.call-start = ((), (), s32[]{:S(2)}) async-start(), calls=%async_computation.20 | async-start | bytes 3145728 | tf_op jit(solution)/shard_map/all_gather | solution.py:35
  418.4 154.2 %reduce-scatter.21.cloned.1.call-start = ((), (), s32[]{:S(2)}) async-start(), calls=%async_computation.21 | async-start | bytes 3145728 | tf_op jit(solution)/shard_map/reduce_scatter | solution.py:43
  422.0 25.1 %copy-start.79 = (bf16[1,1024,3,512]{1,3,2,0:T(8,128)(2,1)}, bf16[1,1024,3,512]{1,3,2,0:T(8,128)(2,1)S(1)}, u32[]{:S(2)}) copy-start(bf16[1,1024,3,512]{1,3,2,0:T(8,128)(2,1)S(1)} %copy.83) | copy-start | bytes 9437188
  533.6 69.3 %reduce-scatter.29.cloned.1.call-start = ((), (), s32[]{:S(2)}) async-start(), calls=%async_computation.29 | async-start | bytes 3145728 | tf_op jit(solution)/shard_map/reduce_scatter | solution.py:43
  570.8 67.4 %all-gather.25.cloned.1.call-start = ((), (), s32[]{:S(2)}) async-start(), calls=%async_computation.22 | async-start | bytes 3145728 | tf_op jit(solution)/shard_map/all_gather | solution.py:35
  576.8 26.1 %copy-start.27 = (f32[512,1024]{1,0:T(8,128)S(1)}, f32[512,1024]{1,0:T(8,128)}, u32[]{:S(2)}) copy-start(f32[512,1024]{1,0:T(8,128)} %copy-done.26) | copy-start | bytes 6291460
  576.8 96.5 %all-gather.47.cloned.1.call-start = ((), (), s32[]{:S(2)}) async-start(), calls=%async_computation.46 | async-start | bytes 3145728 | tf_op jit(solution)/shard_map/all_gather | solution.py:49
  580.3 128.1 %all-gather.33.cloned.1.call-start = ((), (), s32[]{:S(2)}) async-start(), calls=%async_computation.30 | async-start | bytes 3145728 | tf_op jit(solution)/shard_map/all_gather | solution.py:35
  581.5 23.3 %copy-start.130 = (f32[1,1024]{1,0:T(1,128)}, f32[1,1024]{1,0:T(1,128)S(1)}, u32[]{:S(2)}) copy-start(f32[1,1024]{1,0:T(1,128)S(1)} %fusion.313) | copy-start | bytes 12292
  604.8 44.3 %copy-start.172 = (f32[512]{0:T(512)}, f32[512]{0:T(512)S(1)}, u32[]{:S(2)}) copy-start(f32[512]{0:T(512)S(1)} %multiply_reduce_fusion.4) | copy-start | bytes 6148
  604.8 44.3 %copy-start.150 = (f32[512]{0:T(512)}, f32[512]{0:T(512)S(1)}, u32[]{:S(2)}) copy-start(f32[512]{0:T(512)S(1)} %fusion.334) | copy-start | bytes 6148
  607.2 135.7 %reduce-scatter.33.cloned.1.call-start = ((), (), s32[]{:S(2)}) async-start(), calls=%async_computation.32 | async-start | bytes 3145728 | tf_op jit(solution)/shard_map/reduce_scatter | solution.py:53
  696.0 81.0 %reduce-scatter.23.cloned.1.call-start = ((), (), s32[]{:S(2)}) async-start(), calls=%async_computation.23 | async-start | bytes 3145728 | tf_op jit(solution)/shard_map/reduce_scatter | solution.py:43
  707.2 104.4 %all-gather.49.cloned.1.call-start = ((), (), s32[]{:S(2)}) async-start(), calls=%async_computation.47 | async-start | bytes 3145728 | tf_op jit(solution)/shard_map/all_gather | solution.py:49
  707.8 35.2 %copy-start.39 = (f32[512,1024]{1,0:T(8,128)S(1)}, f32[512,1024]{1,0:T(8,128)}, u32[]{:S(2)}) copy-start(f32[512,1024]{1,0:T(8,128)} %copy-done.38) | copy-start | bytes 6291460
  707.8 139.0 %all-gather.35.cloned.1.call-start = ((), (), s32[]{:S(2)}) async-start(), calls=%async_computation.33 | async-start | bytes 3145728 | tf_op jit(solution)/shard_map/all_gather | solution.py:49
  742.9 34.1 %copy-start.67 = (bf16[512,1024]{1,0:T(8,128)(2,1)S(1)}, bf16[512,1024]{1,0:T(8,128)(2,1)}, u32[]{:S(2)}) copy-start(bf16[512,1024]{1,0:T(8,128)(2,1)} %reduce-scatter.33.cloned.1.call-done) | copy-start | bytes 3145732
  783.1 167.0 %reduce-scatter.41.cloned.1.call-start = ((), (), s32[]{:S(2)}) async-start(), calls=%async_computation.39 | async-start | bytes 3145728 | tf_op jit(solution)/shard_map/reduce_scatter | solution.py:53
  834.2 120.2 %reduce-scatter.31.cloned.1.call-start = ((), (), s32[]{:S(2)}) async-start(), calls=%async_computation.31 | async-start | bytes 3145728 | tf_op jit(solution)/shard_map/reduce_scatter | solution.py:43
  845.4 136.8 %reduce-scatter.35.cloned.1.call-start = ((), (), s32[]{:S(2)}) async-start(), calls=%async_computation.34 | async-start | bytes 3145728 | tf_op jit(solution)/shard_map/reduce_scatter | solution.py:53
  950.1 74.8 %all-gather.41.cloned.1.call-start = ((), (), s32[]{:S(2)}) async-start(), calls=%async_computation.40 | async-start | bytes 3145728 | tf_op jit(solution)/shard_map/all_gather | solution.py:49
  954.3 27.9 %copy-start.25 = (f32[512,1024]{1,0:T(8,128)S(1)}, f32[512,1024]{1,0:T(8,128)}, u32[]{:S(2)}) copy-start(f32[512,1024]{1,0:T(8,128)} %get-tuple-element.937) | copy-start | bytes 6291460
  954.4 27.9 %copy-start.121 = (f32[1,1024]{1,0:T(1,128)S(1)}, f32[1,1024]{1,0:T(1,128)}, u32[]{:S(2)}) copy-start(f32[1,1024]{1,0:T(1,128)} %copy-done.120) | copy-start | bytes 12292
  954.4 27.9 %copy-start.129 = (f32[512]{0:T(512)S(1)}, f32[512]{0:T(512)}, u32[]{:S(2)}) copy-start(f32[512]{0:T(512)} %copy-done.128) | copy-start | bytes 6148
  959.2 25.6 %copy-start.171 = (f32[512]{0:T(512)S(1)}, f32[512]{0:T(512)}, u32[]{:S(2)}) copy-start(f32[512]{0:T(512)} %copy-done.170) | copy-start | bytes 6148
  959.2 25.7 %copy-start.155 = (f32[512]{0:T(512)S(1)}, f32[512]{0:T(512)}, u32[]{:S(2)}) copy-start(f32[512]{0:T(512)} %copy-done.154) | copy-start | bytes 6148
  959.3 28.6 %copy-start.176 = (f32[512]{0:T(512)}, f32[512]{0:T(512)S(1)}, u32[]{:S(2)}) copy-start(f32[512]{0:T(512)S(1)} %negate_multiply_fusion.3) | copy-start | bytes 6148
  959.3 28.6 %copy-start.175 = (f32[512]{0:T(512)S(1)}, f32[512]{0:T(512)}, u32[]{:S(2)}) copy-start(f32[512]{0:T(512)} %copy-done.174) | copy-start | bytes 6148
  991.5 168.5 %reduce-scatter.43.cloned.1.call-start = ((), (), s32[]{:S(2)}) async-start(), calls=%async_computation.41 | async-start | bytes 3145728 | tf_op jit(solution)/shard_map/reduce_scatter | solution.py:53
  991.6 38.5 %copy-start.8 = (bf16[1024,8,64]{0,2,1:T(8,128)(2,1)S(1)}, bf16[1024,8,64]{0,2,1:T(8,128)(2,1)}, u32[]{:S(2)}) copy-start(bf16[1024,8,64]{0,2,1:T(8,128)(2,1)} %copy-done.7) | copy-start | bytes 3145732
  1127.9 66.7 %all-gather.37.cloned.1.call-start = ((), (), s32[]{:S(2)}) async-start(), calls=%async_computation.35 | async-start | bytes 3145728 | tf_op jit(solution)/shard_map/all_gather | solution.py:49
  1149.1 87.5 %all-gather.43.cloned.1.call-start = ((), (), s32[]{:S(2)}) async-start(), calls=%async_computation.42 | async-start | bytes 3145728 | tf_op jit(solution)/shard_map/all_gather | solution.py:49
  1166.8 128.1 %reduce-scatter.37.cloned.1.call-start = ((), (), s32[]{:S(2)}) async-start(), calls=%async_computation.36 | async-start | bytes 3145728 | tf_op jit(solution)/shard_map/reduce_scatter | solution.py:53
  1217.3 80.6 %reduce-scatter.45.cloned.1.call-start = ((), (), s32[]{:S(2)}) async-start(), calls=%async_computation.43 | async-start | bytes 3145728 | tf_op jit(solution)/shard_map/reduce_scatter | solution.py:53
  1260.1 81.0 %all-gather.45.cloned.1.call-start = ((), (), s32[]{:S(2)}) async-start(), calls=%async_computation.44 | async-start | bytes 3145728 | tf_op jit(solution)/shard_map/all_gather | solution.py:49
  1280.6 17.3 copy-start.5
  1280.6 17.3 copy-start.41
  1280.6 17.3 copy-start.133
  1280.6 17.3 copy-start.137
  1280.6 17.3 copy-start.139
  1280.6 17.3 copy-start.147
  1307.9 163.6 %all-gather.39.cloned.1.call-start = ((), (), s32[]{:S(2)}) async-start(), calls=%async_computation.37 | async-start | bytes 3145728 | tf_op jit(solution)/shard_map/all_gather | solution.py:49
  1332.2 310.5 %reduce-scatter.47.cloned.1.call-start = ((), (), s32[]{:S(2)}) async-start(), calls=%async_computation.45 | async-start | bytes 3145728 | tf_op jit(solution)/shard_map/reduce_scatter | solution.py:53
  1471.4 171.4 %reduce-scatter.39.cloned.1.call-start = ((), (), s32[]{:S(2)}) async-start(), calls=%async_computation.38 | async-start | bytes 3145728 | tf_op jit(solution)/shard_map/reduce_scatter | solution.py:53
  1600.5 171.1 %all-reduce.5.cloned.1.call-start = ((), (), s32[]{:S(2)}) async-start(), calls=%async_computation.48 | async-start | bytes 294912 | tf_op jit(solution)/shard_map/psum | solution.py:313
  1649.7 572.6 %all-reduce.7.cloned.1.call-start = ((), (), s32[]{:S(2)}) async-start(), calls=%async_computation.49 | async-start | bytes 50331648 | tf_op jit(solution)/shard_map/psum | solution.py:308
  (219 other events, 1108.4 us)
Sparse Core Ops, SparseCore 0:
  14.3 35.8 all-gather.18
  106.8 31.8 reduce-scatter.16
  142.1 33.1 all-gather.26
  231.9 31.8 reduce-scatter.24
  269.4 33.1 all-gather.28
  304.5 33.1 all-gather.20
  340.5 31.8 reduce-scatter.26
  375.2 31.8 reduce-scatter.18
  413.9 33.1 all-gather.30
  449.0 33.1 all-gather.22
  533.7 31.8 reduce-scatter.20
  570.9 31.9 reduce-scatter.28
  605.0 33.1 all-gather.24
  640.1 33.1 all-gather.46
  675.3 33.1 all-gather.32
  711.1 31.8 reduce-scatter.32
  745.1 31.8 reduce-scatter.22
  778.4 33.1 all-gather.48
  813.7 33.1 all-gather.34
  848.9 31.8 reduce-scatter.40
  883.1 31.8 reduce-scatter.30
  950.2 32.0 reduce-scatter.34
  991.7 33.1 all-gather.40
  1128.0 31.8 reduce-scatter.42
  1161.5 33.1 all-gather.36
  1196.6 33.1 all-gather.42
  1231.8 31.8 reduce-scatter.36
  1266.0 31.8 reduce-scatter.44
  1308.0 33.1 all-gather.44
  1342.6 33.1 all-gather.38
  1471.5 31.8 reduce-scatter.46
  1600.6 31.7 reduce-scatter.38
  1649.8 121.7 all-reduce.4
  1777.0 445.1 all-reduce.6
where the time goes:
time: 2280 us; the launch traced here: 2270 us
  waiting for transfers between devices  1070 us (47%)
  matrix products  689 us (30%)
  other arithmetic  272 us (12%)
  local copies, waits for them, and re-layouts  182 us (8%)
  loops' own time  33.7 us (1%)
    psum x1, waiting for transfers between devices, per_device(): lax.psum(jnp.stack(acc_qkv).astype(jnp.bfloat16), 'dp').astype(jnp.float32)  448 us
    all_gather x8, waiting for transfers between devices, gather_normed(): return lax.all_gather(normed_low, 'tensor', axis=0, tiled=True)  184 us
    reduce_scatter x8, waiting for transfers between devices, sum_branch(): lax.psum_scatter(branch_part.astype(jnp.bfloat16), 'tensor', scatter_dime...  162 us
    dot_general x16, matrix products, block_scores(): jnp.einsum('qhd,khd->hqk', query_block, key_rows, preferred_element_type=...  130 us
    all_gather x8, waiting for transfers between devices, gather_grad(): return lax.all_gather(grad_low, 'tensor', axis=0, tiled=True)  123 us
    psum x1, waiting for transfers between devices, per_device(): lax.psum((jnp.stack(acc_gain), jnp.stack(acc_bias), jnp.stack(acc_scale),...  98 us
    convert_element_type x8, other arithmetic, one_block(): grad_scores = (shares * (grad_shares - inner_sum)).astype(jnp.bfloat16)  83.9 us
    unnamed x413, local copies, waits for them, and re-layouts  63.4 us
  transfers between devices with their start and end apart: 34, of which 25 were waited for; matrix products, arithmetic and copies ran while one was open for 33% of the time, Pallas kernels for 0%

commit v1 on v0

--- a/solution.py
+++ b/solution.py
@@ -305,7 +305,9 @@
         frames_list.append(jnp.stack(out_group))
         grads_list.append(jnp.stack(grad_group))
     total_qkv, total_out, total_up, total_down = (
-        lax.psum(jnp.stack(acc_qkv).astype(jnp.bfloat16), "dp").astype(jnp.float32),
+        jnp.sum(lax.all_gather(jnp.stack(acc_qkv).astype(jnp.bfloat16), "dp"), axis=0).astype(
+            jnp.float32
+        ),
         lax.psum(jnp.stack(acc_out).astype(jnp.bfloat16), "dp").astype(jnp.float32),
         lax.psum(jnp.stack(acc_up).astype(jnp.bfloat16), "dp").astype(jnp.float32),
         lax.psum(jnp.stack(acc_down).astype(jnp.bfloat16), "dp").astype(jnp.float32),

time: 2280 us -> 2670 us (1.17)
  waiting for transfers between devices: 1070 us -> 1430 us
  other arithmetic: 272 us -> 308 us
    all_gather x0 -> x1, waiting for transfers between devices: none -> 457 us  [per_device(): lax.all_gather(jnp.stack(acc_qkv).astype(jnp.bfloat16), 'dp')]
    psum x1, waiting for transfers between devices: 448 us -> 335 us  [per_device(): lax.psum(jnp.stack(acc_out).astype(jnp.bfloat16), 'dp').astype(jnp.float32)]
    reduce_sum x0 -> x1, other arithmetic: none -> 35.2 us  [per_device(): jnp.sum(lax.all_gather(jnp.stack(acc_qkv).astype(jnp.bfloat16), 'dp'), ax...]
    unnamed x413 -> x421, local copies, waits for them, and re-layouts: 63.4 us -> 65.5 us
  transfers between devices with their start and end apart: 34 -> 35, of which waited for: 25 -> 28; matrix products, arithmetic and copies ran while one was open for 33% -> 29% of each run, Pallas kernels for 0% -> 0%
where the time goes in v1:
time: 2670 us; the launch traced here: 2660 us
  waiting for transfers between devices  1430 us (54%)
  matrix products  681 us (26%)
  other arithmetic  308 us (12%)
  local copies, waits for them, and re-layouts  185 us (7%)
  loops' own time  33.6 us (1%)
    all_gather x1, waiting for transfers between devices, per_device(): lax.all_gather(jnp.stack(acc_qkv).astype(jnp.bfloat16), 'dp')  457 us
    psum x1, waiting for transfers between devices, per_device(): lax.psum(jnp.stack(acc_out).astype(jnp.bfloat16), 'dp').astype(jnp.float32)  335 us
    all_gather x8, waiting for transfers between devices, gather_normed(): return lax.all_gather(normed_low, 'tensor', axis=0, tiled=True)  184 us
    reduce_scatter x8, waiting for transfers between devices, sum_branch(): lax.psum_scatter(branch_part.astype(jnp.bfloat16), 'tensor', scatter_dime...  162 us
    all_gather x8, waiting for transfers between devices, gather_grad(): return lax.all_gather(grad_low, 'tensor', axis=0, tiled=True)  134 us
    dot_general x16, matrix products, block_scores(): jnp.einsum('qhd,khd->hqk', query_block, key_rows, preferred_element_type=...  130 us
    convert_element_type x8, other arithmetic, one_block(): grad_scores = (shares * (grad_shares - inner_sum)).astype(jnp.bfloat16)  83.8 us
    psum x1, waiting for transfers between devices, per_device(): lax.psum((jnp.stack(acc_gain), jnp.stack(acc_bias), jnp.stack(acc_scale),...  82.2 us
  transfers between devices with their start and end apart: 35, of which 28 were waited for; matrix products, arithmetic and copies ran while one was open for 29% of the time, Pallas kernels for 0%

profile of v1, /device:TPU:0, one launch (start us, length us, event | category | flops | bytes accessed | tf_op | source)
XLA Modules:
  0.0 2661.1 jit_solution(7391442716260046762)
XLA Ops:
  27.9 22.2 all-gather.20.cloned.1.call-done
  63.6 38.0 %while.108 = (s32[]{:T(128)}, bf16[2,512,8,64]{1,3,2,0:T(8,128)(2,1)S(1)}, f32[2,8,512,1]{2,1,3,0:T(8,128)S(1)}, s32[]{:T(128)}, s32[]{:T(128)}, /*index=5*/s32[...) while((s32[]{:T(128)}, ...), condition=%wide.region_5.6_spmd, body=%wide.region_2.5_spmd.sunk | while | flops 1121712640 | bytes 55713984 | solution.py:103
  107.2 31.4 %reduce-scatter.17.cloned.1.call-done = bf16[512,1024]{1,0:T(8,128)(2,1)} async-done(((bf16[1024,1024]{1,0:T(8,128)(2,1)}), bf16[512,1024]{1,0:T(8,128)(2,1)}) %reduce-scatter.17.cloned.1.call-update) | async-done | bytes 1048592 | tf_op jit(solution)/shard_map/reduce_scatter | solution.py:43
  143.3 31.9 %all-gather.28.cloned.1.call-done = bf16[1024,1024]{1,0:T(8,128)(2,1)} async-done(((bf16[512,1024]{1,0:T(8,128)(2,1)}), bf16[1024,1024]{1,0:T(8,128)(2,1)}) %all-gather.28.cloned.1.call-update) | async-done | bytes 2097168 | tf_op jit(solution)/shard_map/all_gather | solution.py:35
  188.7 37.9 %while.110 = (s32[]{:T(128)}, bf16[2,512,8,64]{1,3,2,0:T(8,128)(2,1)S(1)}, f32[2,8,512,1]{2,1,3,0:T(8,128)S(1)}, s32[]{:T(128)}, s32[]{:T(128)}, /*index=5*/s32[...) while((s32[]{:T(128)}, ...), condition=%wide.region_25.26_spmd, body=%wide.region_22.25_spmd.sunk | while | flops 1121712640 | bytes 55713984 | solution.py:103
  231.8 31.7 %reduce-scatter.25.cloned.1.call-done = bf16[512,1024]{1,0:T(8,128)(2,1)} async-done(((bf16[1024,1024]{1,0:T(8,128)(2,1)}), bf16[512,1024]{1,0:T(8,128)(2,1)}) %reduce-scatter.25.cloned.1.call-update) | async-done | bytes 1048592 | tf_op jit(solution)/shard_map/reduce_scatter | solution.py:43
  269.7 32.6 %all-gather.30.cloned.1.call-done = bf16[1024,1024]{1,0:T(8,128)(2,1)} async-done(((bf16[512,1024]{1,0:T(8,128)(2,1)}), bf16[1024,1024]{1,0:T(8,128)(2,1)}) %all-gather.30.cloned.1.call-update) | async-done | bytes 2097168 | tf_op jit(solution)/shard_map/all_gather | solution.py:35
  322.0 15.4 all-gather.22.cloned.1.call-done
  360.1 12.0 reduce-scatter.27.cloned.1.call-done
  372.1 34.8 %reduce-scatter.19.cloned.1.call-done = bf16[512,1024]{1,0:T(8,128)(2,1)} async-done(((bf16[1024,1024]{1,0:T(8,128)(2,1)}), bf16[512,1024]{1,0:T(8,128)(2,1)}) %reduce-scatter.19.cloned.1.call-update) | async-done | bytes 1048592 | tf_op jit(solution)/shard_map/reduce_scatter | solution.py:43
  422.0 24.8 all-gather.32.cloned.1.call-done
  456.7 25.2 all-gather.24.cloned.1.call-done
  495.6 31.0 %while.109 = (s32[]{:T(128)}, bf16[2,512,8,64]{1,3,2,0:T(8,128)(2,1)}, f32[2,8,512,1]{2,1,3,0:T(8,128)S(1)}, s32[]{:T(128)}, s32[2]{0:T(128)S(1)}, /*index=5*/bf...) while((s32[]{:T(128)}, ...), condition=%wide.region_15.16_spmd, body=%wide.region_12.15_spmd.sunk | while | flops 1120138240 | bytes 66195716 | solution.py:103
  534.7 28.7 %while.111 = (s32[]{:T(128)}, bf16[2,512,8,64]{1,3,2,0:T(8,128)(2,1)}, f32[2,8,512,1]{2,1,3,0:T(8,128)S(1)}, s32[]{:T(128)}, s32[2]{0:T(128)S(1)}, /*index=5*/bf...) while((s32[]{:T(128)}, ...), condition=%wide.region_35.36_spmd, body=%wide.region_32.35_spmd.sunk | while | flops 1120138240 | bytes 62001388 | solution.py:103
  581.6 20.7 reduce-scatter.29.cloned.1.call-done
  606.7 31.0 %all-gather.26.cloned.1.call-done = bf16[1024,1024]{1,0:T(8,128)(2,1)} async-done(((bf16[512,1024]{1,0:T(8,128)(2,1)}), bf16[1024,1024]{1,0:T(8,128)(2,1)}) %all-gather.26.cloned.1.call-update) | async-done | bytes 2097168 | tf_op jit(solution)/shard_map/all_gather | solution.py:35
  637.6 10.9 fusion.158
  648.5 24.2 all-gather.50.cloned.1.call-done
  672.8 12.5 fusion.125
  695.9 11.0 fusion.275
  707.9 11.0 fusion.156
  718.9 23.5 reduce-scatter.33.cloned.1.call-done
  745.1 31.3 %reduce-scatter.23.cloned.1.call-done = bf16[512,1024]{1,0:T(8,128)(2,1)} async-done(((bf16[1024,1024]{1,0:T(8,128)(2,1)}), bf16[512,1024]{1,0:T(8,128)(2,1)}) %reduce-scatter.23.cloned.1.call-update) | async-done | bytes 1048592 | tf_op jit(solution)/shard_map/reduce_scatter | solution.py:43
  782.9 28.1 %all-gather.52.cloned.1.call-done = bf16[1,1,1024,1024]{3,2,1,0:T(8,128)(2,1)} async-done(((bf16[1,1,512,1024]{3,2,1,0:T(8,128)(2,1)}), bf16[1,1,1024,1024]{3,2,1,0:T(8,128)(2,1)}) %all-gather.52.cloned.1.call-update) | async-done | bytes 2097168 | tf_op jit(solution)/shard_map/all_gather | solution.py:49
  811.0 12.5 fusion.139
  833.7 11.1 fusion.278
  851.2 86.7 %while.112 = (s32[]{:T(128)}, f32[1024,8,64]{0,2,1:T(8,128)}, f32[1024,8,64]{0,2,1:T(8,128)}, bf16[2,512,8,64]{1,3,2,0:T(8,128)(2,1)}, s32[2]{0:T(128)S(1)}, /*i...) while((s32[]{:T(128)}, f32[1024,8,64]{0,2,1:T(8,128)}, ...), condition=%wide.region_45.46_spmd.clone, body=%wide.region_43.45_spmd.clone.sunk | while | flops 2724983808 | bytes 207702432 | solution.py:145
  859.2 10.8 multiply_reduce_fusion.14
  902.1 10.8 multiply_reduce_fusion.14
  958.8 23.1 reduce-scatter.35.cloned.1.call-done
  991.2 33.2 %all-gather.42.cloned.1.call-done = bf16[1024,1024]{1,0:T(8,128)(2,1)} async-done(((bf16[512,1024]{1,0:T(8,128)(2,1)}), bf16[1024,1024]{1,0:T(8,128)(2,1)}) %all-gather.42.cloned.1.call-update) | async-done | bytes 2097168 | tf_op jit(solution)/shard_map/all_gather | solution.py:49
  1029.6 86.6 %while.114 = (s32[]{:T(128)}, f32[1024,8,64]{0,2,1:T(8,128)}, f32[1024,8,64]{0,2,1:T(8,128)}, bf16[2,512,8,64]{1,3,2,0:T(8,128)(2,1)}, s32[2]{0:T(128)S(1)}, /*i...) while((s32[]{:T(128)}, f32[1024,8,64]{0,2,1:T(8,128)}, ...), condition=%wide.region_63.64_spmd.clone, body=%wide.region_61.63_spmd.clone.sunk | while | flops 2724983808 | bytes 207702432 | solution.py:145
  1037.6 10.8 multiply_reduce_fusion.16
  1080.4 10.8 multiply_reduce_fusion.16
  1129.0 10.9 fusion.382
  1140.0 19.6 reduce-scatter.43.cloned.1.call-done
  1166.3 27.9 %all-gather.38.cloned.1.call-done = bf16[1024,1024]{1,0:T(8,128)(2,1)} async-done(((bf16[512,1024]{1,0:T(8,128)(2,1)}), bf16[1024,1024]{1,0:T(8,128)(2,1)}) %all-gather.38.cloned.1.call-update) | async-done | bytes 2097168 | tf_op jit(solution)/shard_map/all_gather | solution.py:49
  1194.3 12.7 fusion.118
  1217.4 10.1 fusion.141
  1228.8 12.5 fusion.132
  1251.9 12.8 fusion.254
  1264.7 14.1 fusion.143
  1321.8 18.3 all-gather.46.cloned.1.call-done
  1345.0 114.4 %while.115 = (s32[]{:T(128)}, f32[1024,8,64]{0,2,1:T(8,128)}, f32[1024,8,64]{0,2,1:T(8,128)}, bf16[2,512,8,64]{1,3,2,0:T(8,128)(2,1)}, s32[2]{0:T(128)S(1)}, /*i...) while((s32[]{:T(128)}, f32[1024,8,64]{0,2,1:T(8,128)}, ...), condition=%wide.region_72.73_spmd.clone, body=%wide.region_70.72_spmd.clone.sunk | while | flops 2726558208 | bytes 225534288 | solution.py:145
  1349.7 10.2 fusion.588
  1360.0 13.5 multiply_reduce_fusion.17
  1373.4 11.5 multiply_convert_fusion.23
  1416.4 13.5 multiply_reduce_fusion.17
  1429.9 11.5 multiply_convert_fusion.23
  1475.1 114.4 %while.113 = (s32[]{:T(128)}, f32[1024,8,64]{0,2,1:T(8,128)}, f32[1024,8,64]{0,2,1:T(8,128)}, bf16[2,512,8,64]{1,3,2,0:T(8,128)(2,1)}, s32[2]{0:T(128)S(1)}, /*i...) while((s32[]{:T(128)}, f32[1024,8,64]{0,2,1:T(8,128)}, ...), condition=%wide.region_54.55_spmd.clone, body=%wide.region_52.54_spmd.clone.sunk | while | flops 2726558208 | bytes 225534288 | solution.py:145
  1479.4 10.1 fusion.565
  1489.5 13.6 multiply_reduce_fusion.15
  1503.1 11.5 multiply_convert_fusion.21
  1536.2 10.0 fusion.565
  1546.2 13.5 multiply_reduce_fusion.15
  1559.7 11.5 multiply_convert_fusion.21
  1600.2 14.1 fusion.142
  1689.3 82.2 %all-reduce.5.cloned.1.call-done = (f32[2,1024]{1,0:T(2,128)}, f32[2,1024]{1,0:T(2,128)}, f32[2,7,1024]{2,1,0:T(8,128)}, f32[2,7,1024]{2,1,0:T(8,128)}) async-done(((f32[2,1024]{1,0:T(2,128)}, f32[2,1024]{1,0:T(2,128)}, f32[2,7,1024]{2,1,0:T(8,128)}, f32[2,7,1024]{2,1,0:T(8,128)}), (f32[2,1024]{1,0:T(2,128)}, f32[2,1024]{1,0:T(2,128)}, f32[2,7,1024]{2,1,0:T(8,128)}, ...) | async-done | bytes 131088 | tf_op jit(solution)/shard_map/psum | solution.py:315
  1774.6 335.1 %all-reduce.7.cloned.1.call-done = (bf16[2,512,1024]{2,1,0:T(8,128)(2,1)}, bf16[2,1024,2048]{2,1,0:T(8,128)(2,1)}, bf16[2,2048,1024]{2,1,0:T(8,128)(2,1)}) async-done(((bf16[2,512,1024]{2,1,0:T(8,128)(2,1)}, bf16[2,1024,2048]{2,1,0:T(8,128)(2,1)}, bf16[2,2048,1024]{2,1,0:T(8,128)(2,1)}), (bf16[2,512,1024]{2,1,0:T(8,128)(2,1)}, bf16[2,1024,2048]{2,1,0:T(8,128)(2,1)}, ...) | async-done | bytes 18874384 | tf_op jit(solution)/shard_map/psum | solution.py:311
  2113.8 13.1 convert_element_type.372
  2126.8 11.7 convert_element_type.373
  2138.5 457.1 %all-gather.48.cloned.1.call-done = bf16[16,2,1024,1536]{3,2,1,0:T(8,128)(2,1)} async-done(((bf16[1,2,1024,1536]{3,2,1,0:T(8,128)(2,1)}), bf16[16,2,1024,1536]{3,2,1,0:T(8,128)(2,1)}) %all-gather.48.cloned.1.call-update) | async-done | bytes 100663312 | tf_op jit(solution)/shard_map/all_gather | solution.py:308
  2595.6 35.2 %reduce_sum.568 = bf16[2,1024,1536]{2,1,0:T(8,128)(2,1)} reduce(bf16[16,2,1024,1536]{3,2,1,0:T(8,128)(2,1)} %all-gather.48.cloned.1.call-done, bf16[]{:T(256)} %constant.201.clone.1), dimensions={0}, to_apply=%region_76.77 | reduce | flops 47185920 | bytes 106954752 | tf_op jit(solution)/shard_map/reduce_sum | solution.py:308
  2640.2 12.6 copy.105
  (914 shorter events, 787.4 us)
Async XLA Ops:
  7.2 42.9 %all-gather.20.cloned.1.call-start = ((), (), s32[]{:S(2)}) async-start(), calls=%async_computation.16 | async-start | bytes 3145728 | tf_op jit(solution)/shard_map/all_gather | solution.py:35
  12.1 128.3 %copy-start.120 = (f32[1,1024]{1,0:T(1,128)}, f32[1,1024]{1,0:T(1,128)S(1)}, u32[]{:S(2)}) copy-start(f32[1,1024]{1,0:T(1,128)S(1)} %get-tuple-element.1007) | copy-start | bytes 12292
  14.2 124.4 %reduce-scatter.17.cloned.1.call-start = ((), (), s32[]{:S(2)}) async-start(), calls=%async_computation.17 | async-start | bytes 3145728 | tf_op jit(solution)/shard_map/reduce_scatter | solution.py:43
  106.6 68.6 %all-gather.28.cloned.1.call-start = ((), (), s32[]{:S(2)}) async-start(), calls=%async_computation.24 | async-start | bytes 3145728 | tf_op jit(solution)/shard_map/all_gather | solution.py:35
  107.1 34.8 %copy-start.128 = (f32[512]{0:T(512)}, f32[512]{0:T(512)S(1)}, u32[]{:S(2)}) copy-start(f32[512]{0:T(512)S(1)} %broadcast_multiply_fusion.3) | copy-start | bytes 6148
  140.4 34.8 %copy-start.168 = (f32[512]{0:T(512)}, f32[512]{0:T(512)S(1)}, u32[]{:S(2)}) copy-start(f32[512]{0:T(512)S(1)} %get-tuple-element.743) | copy-start | bytes 6148
  140.5 34.7 %copy-start.148 = (f32[512]{0:T(512)}, f32[512]{0:T(512)S(1)}, u32[]{:S(2)}) copy-start(f32[512]{0:T(512)S(1)} %fusion.331) | copy-start | bytes 6148
  141.9 121.6 %reduce-scatter.25.cloned.1.call-start = ((), (), s32[]{:S(2)}) async-start(), calls=%async_computation.25 | async-start | bytes 3145728 | tf_op jit(solution)/shard_map/reduce_scatter | solution.py:43
  228.9 34.6 %copy-start.40 = (bf16[512,1024]{1,0:T(8,128)(2,1)S(1)}, bf16[512,1024]{1,0:T(8,128)(2,1)}, u32[]{:S(2)}) copy-start(bf16[512,1024]{1,0:T(8,128)(2,1)} %reduce-scatter.17.cloned.1.call-done) | copy-start | bytes 3145732
  231.6 70.8 %all-gather.30.cloned.1.call-start = ((), (), s32[]{:S(2)}) async-start(), calls=%async_computation.26 | async-start | bytes 3145728 | tf_op jit(solution)/shard_map/all_gather | solution.py:35
  231.8 35.0 %copy-start.140 = (f32[512]{0:T(512)}, f32[512]{0:T(512)S(1)}, u32[]{:S(2)}) copy-start(f32[512]{0:T(512)S(1)} %broadcast_multiply_fusion.6) | copy-start | bytes 6148
  231.8 35.0 %copy-start.136 = (f32[1,1024]{1,0:T(1,128)S(1)}, f32[1,1024]{1,0:T(1,128)}, u32[]{:S(2)}) copy-start(f32[1,1024]{1,0:T(1,128)} %get-tuple-element.1006) | copy-start | bytes 12292
  231.8 35.0 %copy-start.192 = (f32[1,1024]{1,0:T(1,128)S(1)}, f32[1,1024]{1,0:T(1,128)}, u32[]{:S(2)}) copy-start(f32[1,1024]{1,0:T(1,128)} %get-tuple-element.1008) | copy-start | bytes 12292
  269.0 68.4 %all-gather.22.cloned.1.call-start = ((), (), s32[]{:S(2)}) async-start(), calls=%async_computation.18 | async-start | bytes 3145728 | tf_op jit(solution)/shard_map/all_gather | solution.py:35
  269.6 102.5 %reduce-scatter.27.cloned.1.call-start = ((), (), s32[]{:S(2)}) async-start(), calls=%async_computation.27 | async-start | bytes 3145728 | tf_op jit(solution)/shard_map/reduce_scatter | solution.py:43
  321.7 85.2 %reduce-scatter.19.cloned.1.call-start = ((), (), s32[]{:S(2)}) async-start(), calls=%async_computation.19 | async-start | bytes 3145728 | tf_op jit(solution)/shard_map/reduce_scatter | solution.py:43
  356.6 90.2 %all-gather.32.cloned.1.call-start = ((), (), s32[]{:S(2)}) async-start(), calls=%async_computation.28 | async-start | bytes 3145728 | tf_op jit(solution)/shard_map/all_gather | solution.py:35
  358.7 52.6 %copy-start.122 = (f32[1,1024]{1,0:T(1,128)}, f32[1,1024]{1,0:T(1,128)S(1)}, u32[]{:S(2)}) copy-start(f32[1,1024]{1,0:T(1,128)S(1)} %fusion.317) | copy-start | bytes 12292
  413.5 68.4 %all-gather.24.cloned.1.call-start = ((), (), s32[]{:S(2)}) async-start(), calls=%async_computation.20 | async-start | bytes 3145728 | tf_op jit(solution)/shard_map/all_gather | solution.py:35
  418.1 154.1 %reduce-scatter.21.cloned.1.call-start = ((), (), s32[]{:S(2)}) async-start(), calls=%async_computation.21 | async-start | bytes 3145728 | tf_op jit(solution)/shard_map/reduce_scatter | solution.py:43
  422.0 24.8 copy-start.80
  533.2 69.1 %reduce-scatter.29.cloned.1.call-start = ((), (), s32[]{:S(2)}) async-start(), calls=%async_computation.29 | async-start | bytes 3145728 | tf_op jit(solution)/shard_map/reduce_scatter | solution.py:43
  570.4 67.3 %all-gather.26.cloned.1.call-start = ((), (), s32[]{:S(2)}) async-start(), calls=%async_computation.22 | async-start | bytes 3145728 | tf_op jit(solution)/shard_map/all_gather | solution.py:35
  576.4 26.0 copy-start.27
  576.4 96.4 %all-gather.50.cloned.1.call-start = ((), (), s32[]{:S(2)}) async-start(), calls=%async_computation.47 | async-start | bytes 3145728 | tf_op jit(solution)/shard_map/all_gather | solution.py:49
  579.8 128.1 %all-gather.34.cloned.1.call-start = ((), (), s32[]{:S(2)}) async-start(), calls=%async_computation.30 | async-start | bytes 3145728 | tf_op jit(solution)/shard_map/all_gather | solution.py:35
  580.8 23.4 copy-start.134
  604.2 44.3 %copy-start.176 = (f32[512]{0:T(512)}, f32[512]{0:T(512)S(1)}, u32[]{:S(2)}) copy-start(f32[512]{0:T(512)S(1)} %multiply_reduce_fusion.4) | copy-start | bytes 6148
  604.3 44.3 %copy-start.154 = (f32[512]{0:T(512)}, f32[512]{0:T(512)S(1)}, u32[]{:S(2)}) copy-start(f32[512]{0:T(512)S(1)} %fusion.334) | copy-start | bytes 6148
  606.6 135.8 %reduce-scatter.33.cloned.1.call-start = ((), (), s32[]{:S(2)}) async-start(), calls=%async_computation.32 | async-start | bytes 3145728 | tf_op jit(solution)/shard_map/reduce_scatter | solution.py:53
  695.4 81.0 %reduce-scatter.23.cloned.1.call-start = ((), (), s32[]{:S(2)}) async-start(), calls=%async_computation.23 | async-start | bytes 3145728 | tf_op jit(solution)/shard_map/reduce_scatter | solution.py:43
  706.9 104.1 %all-gather.52.cloned.1.call-start = ((), (), s32[]{:S(2)}) async-start(), calls=%async_computation.48 | async-start | bytes 3145728 | tf_op jit(solution)/shard_map/all_gather | solution.py:49
  707.5 34.9 %copy-start.39 = (f32[512,1024]{1,0:T(8,128)S(1)}, f32[512,1024]{1,0:T(8,128)}, u32[]{:S(2)}) copy-start(f32[512,1024]{1,0:T(8,128)} %copy-done.38) | copy-start | bytes 6291460
  707.5 138.8 %all-gather.36.cloned.1.call-start = ((), (), s32[]{:S(2)}) async-start(), calls=%async_computation.33 | async-start | bytes 3145728 | tf_op jit(solution)/shard_map/all_gather | solution.py:49
  742.4 34.1 %copy-start.66 = (bf16[512,1024]{1,0:T(8,128)(2,1)S(1)}, bf16[512,1024]{1,0:T(8,128)(2,1)}, u32[]{:S(2)}) copy-start(bf16[512,1024]{1,0:T(8,128)(2,1)} %reduce-scatter.33.cloned.1.call-done) | copy-start | bytes 3145732
  782.7 167.0 %reduce-scatter.41.cloned.1.call-start = ((), (), s32[]{:S(2)}) async-start(), calls=%async_computation.39 | async-start | bytes 3145728 | tf_op jit(solution)/shard_map/reduce_scatter | solution.py:53
  833.7 120.3 %reduce-scatter.31.cloned.1.call-start = ((), (), s32[]{:S(2)}) async-start(), calls=%async_computation.31 | async-start | bytes 3145728 | tf_op jit(solution)/shard_map/reduce_scatter | solution.py:43
  844.9 136.9 %reduce-scatter.35.cloned.1.call-start = ((), (), s32[]{:S(2)}) async-start(), calls=%async_computation.34 | async-start | bytes 3145728 | tf_op jit(solution)/shard_map/reduce_scatter | solution.py:53
  949.6 74.8 %all-gather.42.cloned.1.call-start = ((), (), s32[]{:S(2)}) async-start(), calls=%async_computation.40 | async-start | bytes 3145728 | tf_op jit(solution)/shard_map/all_gather | solution.py:49
  953.9 28.0 %copy-start.25 = (f32[512,1024]{1,0:T(8,128)S(1)}, f32[512,1024]{1,0:T(8,128)}, u32[]{:S(2)}) copy-start(f32[512,1024]{1,0:T(8,128)} %get-tuple-element.946) | copy-start | bytes 6291460
  953.9 28.0 %copy-start.125 = (f32[1,1024]{1,0:T(1,128)S(1)}, f32[1,1024]{1,0:T(1,128)}, u32[]{:S(2)}) copy-start(f32[1,1024]{1,0:T(1,128)} %copy-done.124) | copy-start | bytes 12292
  953.9 28.0 %copy-start.133 = (f32[512]{0:T(512)S(1)}, f32[512]{0:T(512)}, u32[]{:S(2)}) copy-start(f32[512]{0:T(512)} %copy-done.132) | copy-start | bytes 6148
  958.7 25.8 copy-start.175
  958.7 25.8 copy-start.159
  958.7 28.7 %copy-start.180 = (f32[512]{0:T(512)}, f32[512]{0:T(512)S(1)}, u32[]{:S(2)}) copy-start(f32[512]{0:T(512)S(1)} %negate_multiply_fusion.3) | copy-start | bytes 6148
  958.8 28.7 %copy-start.179 = (f32[512]{0:T(512)S(1)}, f32[512]{0:T(512)}, u32[]{:S(2)}) copy-start(f32[512]{0:T(512)} %copy-done.178) | copy-start | bytes 6148
  991.2 168.4 %reduce-scatter.43.cloned.1.call-start = ((), (), s32[]{:S(2)}) async-start(), calls=%async_computation.41 | async-start | bytes 3145728 | tf_op jit(solution)/shard_map/reduce_scatter | solution.py:53
  991.2 38.4 %copy-start.8 = (bf16[1024,8,64]{0,2,1:T(8,128)(2,1)S(1)}, bf16[1024,8,64]{0,2,1:T(8,128)(2,1)}, u32[]{:S(2)}) copy-start(bf16[1024,8,64]{0,2,1:T(8,128)(2,1)} %copy-done.7) | copy-start | bytes 3145732
  1127.6 66.7 %all-gather.38.cloned.1.call-start = ((), (), s32[]{:S(2)}) async-start(), calls=%async_computation.35 | async-start | bytes 3145728 | tf_op jit(solution)/shard_map/all_gather | solution.py:49
  1129.0 30.6 %copy-start.28 = (f32[512,1024]{1,0:T(8,128)S(1)}, f32[512,1024]{1,0:T(8,128)}, u32[]{:S(2)}) copy-start(f32[512,1024]{1,0:T(8,128)} %copy-done.26) | copy-start | bytes 6291460
  1129.0 30.6 %copy-start.123 = (f32[1,1024]{1,0:T(1,128)S(1)}, f32[1,1024]{1,0:T(1,128)}, u32[]{:S(2)}) copy-start(f32[1,1024]{1,0:T(1,128)} %copy-done.122) | copy-start | bytes 12292
  1129.0 30.6 %copy-start.131 = (f32[512]{0:T(512)S(1)}, f32[512]{0:T(512)}, u32[]{:S(2)}) copy-start(f32[512]{0:T(512)} %copy-done.130) | copy-start | bytes 6148
  1129.0 99.8 %all-gather.44.cloned.1.call-start = ((), (), s32[]{:S(2)}) async-start(), calls=%async_computation.42 | async-start | bytes 3145728 | tf_op jit(solution)/shard_map/all_gather | solution.py:49
  1140.0 24.0 copy-start.181
  1166.3 123.0 %reduce-scatter.37.cloned.1.call-start = ((), (), s32[]{:S(2)}) async-start(), calls=%async_computation.36 | async-start | bytes 3145728 | tf_op jit(solution)/shard_map/reduce_scatter | solution.py:53
  1217.3 79.6 %reduce-scatter.45.cloned.1.call-start = ((), (), s32[]{:S(2)}) async-start(), calls=%async_computation.43 | async-start | bytes 3145728 | tf_op jit(solution)/shard_map/reduce_scatter | solution.py:53
  1251.6 88.4 %all-gather.46.cloned.1.call-start = ((), (), s32[]{:S(2)}) async-start(), calls=%async_computation.44 | async-start | bytes 3145728 | tf_op jit(solution)/shard_map/all_gather | solution.py:49
  1251.9 29.5 %slice-start = ((s8[8388608]{0:T(1024)(128)(4,1)}), s8[4194304]{0:T(1024)(128)(4,1)S(1)}, s32[]{:S(2)}) async-start(s8[8388608]{0:T(1024)(128)(4,1)} %bitcast.742), calls=%async_computation.51 | async-start | bytes 8388608
  1306.8 163.2 %all-gather.40.cloned.1.call-start = ((), (), s32[]{:S(2)}) async-start(), calls=%async_computation.37 | async-start | bytes 3145728 | tf_op jit(solution)/shard_map/all_gather | solution.py:49
  1321.7 321.1 %reduce-scatter.47.cloned.1.call-start = ((), (), s32[]{:S(2)}) async-start(), calls=%async_computation.45 | async-start | bytes 3145728 | tf_op jit(solution)/shard_map/reduce_scatter | solution.py:53
  1470.0 172.9 %reduce-scatter.39.cloned.1.call-start = ((), (), s32[]{:S(2)}) async-start(), calls=%async_computation.38 | async-start | bytes 3145728 | tf_op jit(solution)/shard_map/reduce_scatter | solution.py:53
  1600.2 171.4 %all-reduce.5.cloned.1.call-start = ((), (), s32[]{:S(2)}) async-start(), calls=%async_computation.49 | async-start | bytes 294912 | tf_op jit(solution)/shard_map/psum | solution.py:315
  1649.7 460.0 %all-reduce.7.cloned.1.call-start = ((), (), s32[]{:S(2)}) async-start(), calls=%async_computation.50 | async-start | bytes 37748736 | tf_op jit(solution)/shard_map/psum | solution.py:311
  1652.9 942.8 %all-gather.48.cloned.1.call-start = ((), (), s32[]{:S(2)}) async-start(), calls=%async_computation.46 | async-start | bytes 106954752 | tf_op jit(solution)/shard_map/all_gather | solution.py:308
  (224 other events, 1218.5 us)
Sparse Core Ops, SparseCore 0:
  14.3 35.8 all-gather.19
  106.7 31.8 reduce-scatter.16
  142.0 33.1 all-gather.27
  231.7 31.8 reduce-scatter.24
  269.2 33.1 all-gather.29
  304.3 33.1 all-gather.21
  340.3 31.8 reduce-scatter.26
  375.0 31.8 reduce-scatter.18
  413.6 33.1 all-gather.31
  448.8 33.1 all-gather.23
  533.3 31.8 reduce-scatter.20
  570.5 31.8 reduce-scatter.28
  604.5 33.1 all-gather.25
  639.6 33.1 all-gather.49
  674.7 33.1 all-gather.33
  710.6 31.8 reduce-scatter.32
  744.6 31.8 reduce-scatter.22
  777.9 33.1 all-gather.51
  813.1 33.1 all-gather.35
  848.4 31.8 reduce-scatter.40
  882.6 31.8 reduce-scatter.30
  949.7 32.0 reduce-scatter.34
  991.3 33.1 all-gather.41
  1127.7 31.8 reduce-scatter.42
  1161.1 33.1 all-gather.37
  1195.7 33.1 all-gather.43
  1230.9 31.8 reduce-scatter.36
  1265.1 31.8 reduce-scatter.44
  1306.9 33.1 all-gather.45
  1341.5 33.1 all-gather.39
  1470.1 31.7 reduce-scatter.46
  1600.3 31.8 reduce-scatter.38
  1649.9 121.6 all-reduce.4
  1776.6 333.0 all-reduce.6
  2111.4 484.2 all-gather.47
